TPU v7x, 256 devices: a whole 4x4x8 slice. The times are simulated.
256 devices in a mesh: section: 2 (over core), ctx: 32 (over z, x), mp: 4 (over y).
Axes of the slice: x: 4, y: 4, z: 8, core: 2. Of those that a mesh axis runs over, the one named last changes fastest.
Arguments:
- hidden: bfloat16 [2, 4096, 4672], P('section', 'ctx', 'mp'), may hold values from -120 to 120
- query: bfloat16 [2, 4096, 2048], P('section', 'ctx', 'mp'), may hold values from -6 to 6
- keys: bfloat16 [2, 4096, 2048], P('section', 'ctx', 'mp'), may hold values from -100 to 100
- values: bfloat16 [2, 4096, 2048], P('section', 'ctx', 'mp'), may hold values from -12 to 12
- w_out: bfloat16 [2, 4672, 2048], P('section', 'ctx', 'mp'), may hold values from -0.125 to 0.125
Outputs:
- handed: bfloat16 [2, 4096, 4672], P('section', 'ctx', 'mp')
- context: bfloat16 [2, 4096, 2048], P('section', 'ctx', 'mp')
All inputs are finite; a program needn't handle non-finite values.
Results may differ from a plain program's by a relative error of at most 0.0075.
Values may be sent and summed in bfloat16 or wider, within the bound.
No kernel may reach another device: no remote copies, remote signals or barrier semaphores. Data moves between devices by JAX's collectives and lax.ppermute only.
A program may use at most 128 MiB of HBM per device.

v0:
```python
import jax
import jax.numpy as jnp
from jax import lax
from jax.sharding import PartitionSpec as P

HEAD_DIM = 64


def from_behind(block, axis, distance):
    devices = range(lax.axis_size(axis))
    route = [((i - distance) % len(devices), i) for i in devices]
    return lax.ppermute(block, axis, route)


def head_scores(query_h, keys_h):
    return jnp.einsum("qd,kd->qk", query_h, keys_h, preferred_element_type=jnp.float32)


def body(hidden, query, keys, values, w_out):
    rows = hidden[0]
    query_rows = query[0]
    inner_dev = query_rows.shape[1]
    heads_dev = inner_dev // HEAD_DIM
    keys_local = keys[0]
    values_local = values[0]
    keys_all, values_all = (
        lax.all_gather(keys_local, "ctx", axis=0, tiled=True),
        lax.all_gather(values_local, "ctx", axis=0, tiled=True),
    )
    pieces = []
    for head in range(heads_dev):
        lower = head * HEAD_DIM
        upper = lower + HEAD_DIM
        scores = head_scores(query_rows[:, lower:upper], keys_all[:, lower:upper])
        peak = jnp.max(scores, axis=1, keepdims=True)
        expo = jnp.exp(scores - peak)
        total = jnp.sum(expo, axis=1, keepdims=True)
        summed = jnp.dot(
            expo.astype(jnp.bfloat16),
            values_all[:, lower:upper],
            preferred_element_type=jnp.float32,
        )
        pieces.append(summed / total)
    context = jnp.concatenate(pieces, axis=1).astype(jnp.bfloat16)
    out_local = w_out[0]
    branch_terms = jnp.einsum(
        "ri,di->rd",
        context,
        lax.all_gather(out_local, "ctx", axis=0, tiled=True),
        preferred_element_type=jnp.float32,
    )
    branch = lax.psum_scatter(
        branch_terms.astype(jnp.bfloat16), "mp", scatter_dimension=1, tiled=True
    ).astype(jnp.float32)
    result = (rows.astype(jnp.float32) + branch).astype(jnp.bfloat16)
    handed = from_behind(result, "section", 1)
    return (handed[None], context[None])


def solution(mesh):
    in_specs = (
        P("section", "ctx", "mp"),
        P("section", "ctx", "mp"),
        P("section", "ctx", "mp"),
        P("section", "ctx", "mp"),
        P("section", "ctx", "mp"),
    )
    out_specs = (P("section", "ctx", "mp"), P("section", "ctx", "mp"))
    return jax.shard_map(body, mesh=mesh, in_specs=in_specs, out_specs=out_specs, check_vma=False)
```

profile of v0, /device:TPU:1, one launch (start us, length us, event | category | flops | bytes accessed | tf_op | source)
XLA Modules:
  0.0 321.6 jit_solution(12413351099440571113)
XLA Ops:
  8.7 1.9 copy.10
  10.6 82.0 %all-gather.7.cloned.1.call-done = bf16[1,4096,512]{2,1,0:T(8,128)(2,1)} async-done(((bf16[1,128,512]{2,1,0:T(8,128)(2,1)}), bf16[1,4096,512]{2,1,0:T(8,128)(2,1)}) %all-gather.7.cloned.1.call-update) | async-done | bytes 4194320 | tf_op jit(solution)/shard_map/all_gather | solution.py:27
  92.6 1.8 fusion.75
  94.4 1.3 copy-done.12
  96.1 1.9 fusion.76
  98.0 1.3 copy-done.10
  99.8 1.8 fusion.77
  101.6 1.4 copy-done.8
  103.3 1.9 fusion.78
  105.2 1.4 copy-done.6
  107.0 1.8 fusion.79
  108.8 1.3 copy-done.4
  110.6 1.9 fusion.80
  112.5 1.4 copy-done.2
  114.3 1.8 fusion.81
  116.5 2.2 fusion.82
  119.2 54.6 %all-gather.9.cloned.1.call-done = bf16[1,4096,512]{2,1,0:T(8,128)(2,1)} async-done(((bf16[1,128,512]{2,1,0:T(8,128)(2,1)}), bf16[1,4096,512]{2,1,0:T(8,128)(2,1)}) %all-gather.9.cloned.1.call-update) | async-done | bytes 4194320 | tf_op jit(solution)/shard_map/all_gather | solution.py:28
  173.7 2.6 constant_dynamic-update-slice_fusion.7
  176.4 2.4 constant_dynamic-update-slice_fusion.6
  178.8 2.0 constant_dynamic-update-slice_fusion.5
  180.9 2.4 constant_dynamic-update-slice_fusion.4
  183.3 2.0 constant_dynamic-update-slice_fusion.3
  185.4 2.4 constant_dynamic-update-slice_fusion.2
  187.8 1.9 constant_dynamic-update-slice_fusion.1
  189.7 2.5 constant_dynamic-update-slice_fusion
  192.2 88.1 %all-gather.11.cloned.1.call-done = bf16[1,4672,512]{2,0,1:T(2,128)(2,1)} async-done(((bf16[1,146,512]{2,0,1:T(2,128)(2,1)}), bf16[1,4672,512]{2,0,1:T(2,128)(2,1)}) %all-gather.11.cloned.1.call-update) | async-done | bytes 4784144 | tf_op jit(solution)/shard_map/all_gather | solution.py:49
  280.3 6.2 %convolution_convert_fusion = bf16[128,4672]{0,1:T(8,128)(2,1)} fusion(bf16[128,512]{0,1:T(8,128)(2,1)S(1)} %get-tuple-element.38, bf16[1,4672,512]{2,0,1:T(2,128)(2,1)} %all-gather.11.cloned.1.call-done), kind=kOutput, calls=%fused_computation | convolution fusion | flops 612966400 | bytes 6111232 | tf_op jit(solution)/shard_map/ri,di->rd/dot_general | solution.py:46
  286.6 23.2 %reduce-scatter.2.cloned.1.call-done = bf16[128,1168]{0,1:T(8,128)(2,1)} async-done(((bf16[128,4672]{0,1:T(8,128)(2,1)}), bf16[128,1168]{0,1:T(8,128)(2,1)}) %reduce-scatter.2.cloned.1.call-update) | async-done | bytes 299024 | tf_op jit(solution)/shard_map/reduce_scatter | solution.py:52
  309.8 1.0 fusion.66
  310.8 2.3 collective-permute-start
  313.2 0.8 copy.11
  314.4 0.7 copy.32
  (47 shorter events, 5.6 us)
Async XLA Ops:
  7.2 85.4 %all-gather.7.cloned.1.call-start = ((), (), s32[]{:S(2)}) async-start(), calls=%async_computation.2 | async-start | bytes 4325376 | tf_op jit(solution)/shard_map/all_gather | solution.py:27
  7.9 165.8 %all-gather.9.cloned.1.call-start = ((), (), s32[]{:S(2)}) async-start(), calls=%async_computation.3 | async-start | bytes 4325376 | tf_op jit(solution)/shard_map/all_gather | solution.py:28
  8.6 271.6 %all-gather.11.cloned.1.call-start = ((), (), s32[]{:S(2)}) async-start(), calls=%async_computation.4 | async-start | bytes 9867264 | tf_op jit(solution)/shard_map/all_gather | solution.py:49
  10.6 299.2 %reduce-scatter.2.cloned.1.call-start = ((), (), s32[]{:S(2)}) async-start(), calls=%async_computation.1 | async-start | bytes 1495040 | tf_op jit(solution)/shard_map/reduce_scatter | solution.py:52
  94.4 1.3 copy-start.12
  98.0 1.4 copy-start.10
  101.6 1.4 copy-start.8
  105.2 1.4 copy-start.6
  108.8 1.3 copy-start.4
  112.5 1.4 copy-start.2
  116.1 2.6 copy-start
  173.7 2.6 copy-start.11
  176.4 2.5 copy-start.9
  178.8 2.0 copy-start.7
  180.8 2.5 copy-start.5
  183.3 2.0 copy-start.3
  185.3 2.5 copy-start.1
  280.3 29.5 %copy-start.13 = (bf16[1,128,1168]{1,2,0:T(8,128)(2,1)S(1)}, bf16[1,128,1168]{1,2,0:T(8,128)(2,1)}, u32[]{:S(2)}) copy-start(bf16[1,128,1168]{1,2,0:T(8,128)(2,1)} %param.5) | copy-start | bytes 897028
  310.8 3.6 %collective-permute-start = (bf16[128,1168]{0,1:T(8,128)(2,1)S(1)}, bf16[128,1168]{0,1:T(8,128)(2,1)S(1)}, u32[]{:S(2)}, u32[]{:S(2)}) collective-permute-start(bf16[128,1168]{0,1:T(8,128)(2,1)S(1)} %fusion.66), channel_id=1, source_target_pairs={{128,0},{0,128},{129,1},{1,129},{130,2},{2,130},{131,3},{3,131},{1... | collective-permute-start | bytes 897032 | tf_op jit(solution)/shard_map/ppermute | solution.py:12
Sparse Core Ops, SparseCore 0:
  10.6 81.9 all-gather.6
  95.2 78.5 all-gather.8
  176.9 103.3 all-gather.10
  286.6 23.1 reduce-scatter.1
where the time goes:
time: 322 us
  waiting for transfers between devices  250 us (78%)
  matrix products  39.4 us (12%)
  between operations  14 us (4%)
  local copies, waits for them, and re-layouts  11.6 us (4%)
  other arithmetic  4.54 us (1%)
    all_gather x1, waiting for transfers between devices, body(): lax.all_gather(out_local, 'ctx', axis=0, tiled=True)  88.1 us
    all_gather x1, waiting for transfers between devices, body(): lax.all_gather(keys_local, 'ctx', axis=0, tiled=True)  82 us
    all_gather x1, waiting for transfers between devices, body(): lax.all_gather(values_local, 'ctx', axis=0, tiled=True)  54.6 us
    reduce_scatter x1, waiting for transfers between devices, body(): lax.psum_scatter(branch_terms.astype(jnp.bfloat16), 'mp', scatter_dimensi...  23.2 us
    dot_general x8, matrix products, body(): jnp.dot(expo.astype(jnp.bfloat16), values_all[:, lower:upper], preferred_...  18.3 us
    dot_general x8, matrix products, head_scores(): jnp.einsum('qd,kd->qk', query_h, keys_h, preferred_element_type=jnp.float32)  14.9 us
    unnamed x38, local copies, waits for them, and re-layouts  11.6 us
  transfers between devices with their start and end apart: 5, of which 5 were waited for; matrix products, arithmetic and copies ran while one was open for 12% of the time, Pallas kernels for 0%

commit v1 on v0

--- a/solution.py
+++ b/solution.py
@@ -24,7 +24,9 @@
     keys_local = keys[0]
     values_local = values[0]
     keys_all, values_all = (
-        lax.all_gather(keys_local, "ctx", axis=0, tiled=True),
+        jnp.concatenate(
+            lax.all_to_all(jnp.stack([keys_local] * lax.axis_size("ctx")), "ctx", 0, 0), axis=0
+        ),
         lax.all_gather(values_local, "ctx", axis=0, tiled=True),
     )
     pieces = []

time: 322 us -> 289 us (0.90)
  waiting for transfers between devices: 250 us -> 202 us
  starting transfers between devices: 2.5 us -> 14.6 us
    all_to_all x0 -> x1, waiting for transfers between devices: none -> 117 us  [body(): lax.all_to_all(jnp.stack([keys_local] * lax.axis_size('ctx')), 'ctx', 0, 0)]
    all_gather x1 -> x0, waiting for transfers between devices: 82 us -> none  [body(): lax.all_gather(keys_local, 'ctx', axis=0, tiled=True)]
    all_gather x1, waiting for transfers between devices: 54.6 us -> 0.02 us  [body(): lax.all_gather(values_local, 'ctx', axis=0, tiled=True)]
    all_gather x1, waiting for transfers between devices: 88.1 us -> 61.3 us  [body(): lax.all_gather(out_local, 'ctx', axis=0, tiled=True)]
    all_to_all x0 -> x1, starting transfers between devices: none -> 12.1 us  [body(): lax.all_to_all(jnp.stack([keys_local] * lax.axis_size('ctx')), 'ctx', 0, 0)]
    another operation x0 -> x1, local copies, waits for them, and re-layouts: none -> 3.37 us  [body(): jnp.stack([keys_local] * lax.axis_size('ctx'))]
    unnamed x38 -> x40, local copies, waits for them, and re-layouts: 11.6 us -> 10.7 us
  transfers between devices with their start and end apart: 5 -> 5, of which waited for: 5 -> 4; matrix products, arithmetic and copies ran while one was open for 12% -> 14% of each run, Pallas kernels for 0% -> 0%
where the time goes in v1:
time: 289 us
  waiting for transfers between devices  202 us (70%)
  matrix products  39.4 us (14%)
  starting transfers between devices  14.6 us (5%)
  local copies, waits for them, and re-layouts  14 us (5%)
  between operations  14 us (5%)
  other arithmetic  4.54 us (2%)
    all_to_all x1, waiting for transfers between devices, body(): lax.all_to_all(jnp.stack([keys_local] * lax.axis_size('ctx')), 'ctx', 0, 0)  117 us
    all_gather x1, waiting for transfers between devices, body(): lax.all_gather(out_local, 'ctx', axis=0, tiled=True)  61.3 us
    reduce_scatter x1, waiting for transfers between devices, body(): lax.psum_scatter(branch_terms.astype(jnp.bfloat16), 'mp', scatter_dimensi...  23.2 us
    dot_general x8, matrix products, body(): jnp.dot(expo.astype(jnp.bfloat16), values_all[:, lower:upper], preferred_...  18.3 us
    dot_general x8, matrix products, head_scores(): jnp.einsum('qd,kd->qk', query_h, keys_h, preferred_element_type=jnp.float32)  14.9 us
    all_to_all x1, starting transfers between devices, body(): lax.all_to_all(jnp.stack([keys_local] * lax.axis_size('ctx')), 'ctx', 0, 0)  12.1 us
    unnamed x40, local copies, waits for them, and re-layouts  10.7 us
    dot_general x1, matrix products, body(): jnp.einsum('ri,di->rd', context, lax.all_gather(out_local, 'ctx', axis=0,...  6.19 us
  transfers between devices with their start and end apart: 5, of which 4 were waited for; matrix products, arithmetic and copies ran while one was open for 14% of the time, Pallas kernels for 0%

profile of v1, /device:TPU:1, one launch (start us, length us, event | category | flops | bytes accessed | tf_op | source)
XLA Modules:
  0.0 289.0 jit_solution(15524089712625017005)
XLA Ops:
  7.9 3.4 %stack.3 = bf16[32,128,512]{2,1,0:T(8,128)(2,1)} broadcast(bf16[128,512]{1,0:T(8,128)(2,1)} %bitcast.45), dimensions={1,2} | broadcast | bytes 4325376 | tf_op jit(solution)/shard_map/stack | solution.py:28
  11.3 12.1 %all-to-all-start = ((bf16[32,128,512]{2,1,0:T(8,128)(2,1)}), bf16[32,128,512]{2,1,0:T(8,128)(2,1)}, u32[]{:S(2)}, u32[]{:S(2)}) async-start(bf16[32,128,512]{2,1,0:T(8,128)(2,1)} %stack.3), calls=%async_computation | async-start | bytes 8388608 | tf_op jit(solution)/shard_map/all_to_all | solution.py:28
  23.5 0.9 copy.10
  24.5 116.7 %all-to-all-done = bf16[32,128,512]{2,1,0:T(8,128)(2,1)} async-done(((bf16[32,128,512]{2,1,0:T(8,128)(2,1)}), bf16[32,128,512]{2,1,0:T(8,128)(2,1)}, u32[]{:S(2)}, u32[]{:S(2)}) %all-to-all-start) | async-done | bytes 4194336 | tf_op jit(solution)/shard_map/all_to_all | solution.py:28
  141.2 1.8 fusion.75
  142.9 1.3 copy-done.12
  144.7 1.9 fusion.76
  146.6 1.3 copy-done.10
  148.4 1.8 fusion.77
  150.1 1.4 copy-done.8
  151.9 1.9 fusion.78
  153.8 1.4 copy-done.6
  155.6 1.8 fusion.79
  157.4 1.3 copy-done.4
  159.2 1.9 fusion.80
  161.1 1.4 copy-done.2
  162.9 1.8 fusion.81
  165.2 2.1 fusion.82
  167.8 2.6 constant_dynamic-update-slice_fusion.7
  170.5 2.4 constant_dynamic-update-slice_fusion.6
  172.9 2.0 constant_dynamic-update-slice_fusion.5
  175.0 2.4 constant_dynamic-update-slice_fusion.4
  177.4 2.0 constant_dynamic-update-slice_fusion.3
  179.5 2.4 constant_dynamic-update-slice_fusion.2
  181.9 1.9 constant_dynamic-update-slice_fusion.1
  183.8 2.5 constant_dynamic-update-slice_fusion
  186.3 61.3 %all-gather.7.cloned.1.call-done = bf16[1,4672,512]{2,0,1:T(2,128)(2,1)} async-done(((bf16[1,146,512]{2,0,1:T(2,128)(2,1)}), bf16[1,4672,512]{2,0,1:T(2,128)(2,1)}) %all-gather.7.cloned.1.call-update) | async-done | bytes 4784144 | tf_op jit(solution)/shard_map/all_gather | solution.py:51
  247.6 6.2 %convolution_convert_fusion = bf16[128,4672]{0,1:T(8,128)(2,1)} fusion(bf16[128,512]{0,1:T(8,128)(2,1)S(1)} %get-tuple-element.38, bf16[1,4672,512]{2,0,1:T(2,128)(2,1)} %all-gather.7.cloned.1.call-done), kind=kOutput, calls=%fused_computation | convolution fusion | flops 612966400 | bytes 6111232 | tf_op jit(solution)/shard_map/ri,di->rd/dot_general | solution.py:48
  253.9 23.2 %reduce-scatter.2.cloned.1.call-done = bf16[128,1168]{0,1:T(8,128)(2,1)} async-done(((bf16[128,4672]{0,1:T(8,128)(2,1)}), bf16[128,1168]{0,1:T(8,128)(2,1)}) %reduce-scatter.2.cloned.1.call-update) | async-done | bytes 299024 | tf_op jit(solution)/shard_map/reduce_scatter | solution.py:54
  277.1 1.0 fusion.66
  278.1 2.4 collective-permute-start
  280.5 0.8 copy.11
  (49 shorter events, 5.6 us)
Async XLA Ops:
  7.2 160.6 %all-gather.5.cloned.1.call-start = ((), (), s32[]{:S(2)}) async-start(), calls=%async_computation.3 | async-start | bytes 4325376 | tf_op jit(solution)/shard_map/all_gather | solution.py:30
  11.3 12.2 %copy-start.14 = (bf16[1,146,512]{2,1,0:T(8,128)(2,1)S(1)}, bf16[1,146,512]{2,1,0:T(8,128)(2,1)}, u32[]{:S(2)}) copy-start(bf16[1,146,512]{2,1,0:T(8,128)(2,1)} %param.9) | copy-start | bytes 448516
  11.3 129.9 %all-to-all-start = ((bf16[32,128,512]{2,1,0:T(8,128)(2,1)}), bf16[32,128,512]{2,1,0:T(8,128)(2,1)}, u32[]{:S(2)}, u32[]{:S(2)}) async-start(bf16[32,128,512]{2,1,0:T(8,128)(2,1)} %stack.3), calls=%async_computation | async-start | bytes 8388608 | tf_op jit(solution)/shard_map/all_to_all | solution.py:28
  23.4 224.2 %all-gather.7.cloned.1.call-start = ((), (), s32[]{:S(2)}) async-start(), calls=%async_computation.4 | async-start | bytes 9867264 | tf_op jit(solution)/shard_map/all_gather | solution.py:51
  24.4 252.7 %reduce-scatter.2.cloned.1.call-start = ((), (), s32[]{:S(2)}) async-start(), calls=%async_computation.2 | async-start | bytes 1495040 | tf_op jit(solution)/shard_map/reduce_scatter | solution.py:54
  142.9 1.3 copy-start.12
  146.6 1.4 copy-start.10
  150.1 1.4 copy-start.8
  153.8 1.4 copy-start.6
  157.4 1.3 copy-start.4
  161.1 1.4 copy-start.2
  164.7 2.6 copy-start
  167.8 2.7 copy-start.11
  170.4 2.5 copy-start.9
  172.9 2.0 copy-start.7
  174.9 2.5 copy-start.5
  177.4 2.1 copy-start.3
  179.5 2.5 copy-start.1
  247.6 29.5 %copy-start.13 = (bf16[1,128,1168]{1,2,0:T(8,128)(2,1)S(1)}, bf16[1,128,1168]{1,2,0:T(8,128)(2,1)}, u32[]{:S(2)}) copy-start(bf16[1,128,1168]{1,2,0:T(8,128)(2,1)} %param.5) | copy-start | bytes 897028
  278.1 3.6 %collective-permute-start = (bf16[128,1168]{0,1:T(8,128)(2,1)S(1)}, bf16[128,1168]{0,1:T(8,128)(2,1)S(1)}, u32[]{:S(2)}, u32[]{:S(2)}) collective-permute-start(bf16[128,1168]{0,1:T(8,128)(2,1)S(1)} %fusion.66), channel_id=1, source_target_pairs={{128,0},{0,128},{129,1},{1,129},{130,2},{2,130},{131,3},{3,131},{1... | collective-permute-start | bytes 897032 | tf_op jit(solution)/shard_map/ppermute | solution.py:12
Sparse Core Ops, SparseCore 0:
  10.6 127.7 all-gather.4
  141.5 105.9 all-gather.6
  253.9 23.1 reduce-scatter.1
